TPU v7x, 32 devices: a whole 2x2x4 slice. The times are simulated.
32 devices in a mesh: clip: 2 (over x), seq: 4 (over y, core), sub: 4 (over z).
Axes of the slice: x: 2, y: 2, z: 4, core: 2. Of those that a mesh axis runs over, the one named last changes fastest.
Arguments:
- latent: bfloat16 [4096, 1536], P(('clip', 'seq', 'sub')), parts along dimension 0, may hold values from -6 to 6
- cond_kv: bfloat16 [1024, 2, 1024], P(('clip', 'seq', 'sub')), parts along dimension 0, may hold values from -6 to 6
- qkv_weight: bfloat16 [1536, 3072], replicated, may hold values from -0.15625 to 0.15625
- qk_gain: float32 [2, 16, 64], replicated, may hold values from 0.5 to 16
- out_weight: bfloat16 [1024, 1536], replicated, may hold values from -0.1875 to 0.1875
Outputs:
- output: bfloat16 [4096, 1536], P(('clip', 'seq', 'sub')), parts along dimension 0
There are 2 independent parts, one for each index of `clip`. A program takes and returns all parts, laid end to end along the dimension named above; an argument that names none is the same for every part. Nothing has to cross between parts.
All inputs are finite; a program needn't handle non-finite values.
Results may differ from a plain program's by a relative error of at most 0.008.
The roundings to bfloat16 on the way count: a program that leaves them out, or rounds other values in their place, can miss the bound.
Values may be sent and summed in bfloat16 or wider, within the bound.
A program may use at most 320 MiB of HBM per device.

v0:
```python
import functools

import jax
import jax.numpy as jnp
from jax import lax
from jax.experimental import pallas as pl
from jax.experimental.pallas import tpu as pltpu
from jax.sharding import PartitionSpec as P


def rms_gain(field, gain):
    return field * lax.rsqrt(jnp.mean(field * field, axis=-1, keepdims=True) + 1e-06) * gain


def update(carry, query, key_block, value_block):
    highest, total, summed = carry
    scale = 1.0 / jnp.sqrt(jnp.float32(query.shape[-1]))
    scores = (
        jnp.einsum("qhd,khd->hqk", query, key_block, preferred_element_type=jnp.float32) * scale
    )
    new_high = jnp.maximum(highest, jnp.max(scores, axis=-1))
    expd = jnp.exp(scores - new_high[..., None])
    factor = jnp.exp(highest - new_high)
    total = total * factor + jnp.sum(expd, axis=-1)
    summed = summed * factor[..., None] + jnp.einsum(
        "hqk,khd->hqd", expd.astype(jnp.bfloat16), value_block, preferred_element_type=jnp.float32
    )
    return (new_high, total, summed)


def fold_rows(carry, query, keys_piece, values_piece, block_rows):
    count = keys_piece.shape[0] // block_rows
    key_blocks = keys_piece.reshape((count, block_rows) + keys_piece.shape[1:])
    value_blocks = values_piece.reshape((count, block_rows) + values_piece.shape[1:])

    def advance(state, pair):
        return (update(state, query, pair[0], pair[1]), None)

    carry, unused = lax.scan(advance, carry, (key_blocks, value_blocks))
    return carry


def arrange(sent, cond_sent, width):
    queries = sent.shape[0]
    local_heads = sent.shape[2] // width
    query = sent[:, 0].reshape(queries, local_heads, width)
    keyed = sent[:, 1].reshape(queries, local_heads, width)
    valued = sent[:, 2].reshape(queries, local_heads, width)
    cond_rows = cond_sent.shape[0]
    cond_key = cond_sent[:, 0].reshape(cond_rows, local_heads, width)
    cond_value = cond_sent[:, 1].reshape(cond_rows, local_heads, width)
    start_state = (
        jnp.full((local_heads, queries), -1e30, jnp.float32),
        jnp.zeros((local_heads, queries), jnp.float32),
        jnp.zeros((local_heads, queries, width), jnp.float32),
    )

    def absorb(carry, pieces, start):
        carry = fold_rows(carry, query, pieces[0], pieces[1], queries)
        return fold_rows(carry, query, pieces[2], pieces[3], cond_rows)

    return ((keyed, valued, cond_key, cond_value), start_state, absorb)


def finish(carry):
    highest, total, summed = carry
    attended = summed / total[..., None]
    local_heads, queries, width = attended.shape
    return attended.transpose(1, 0, 2).reshape(queries, local_heads * width).astype(jnp.bfloat16)


def local(latent, cond_kv, qkv_weight, qk_gain, out_weight):
    rows = latent.shape[0]
    heads = qk_gain.shape[1]
    width = qk_gain.shape[2]
    proj = jnp.dot(latent, qkv_weight, preferred_element_type=jnp.float32).reshape(
        rows, 3, heads, width
    )
    query = rms_gain(proj[:, 0], qk_gain[0])
    keyed = rms_gain(proj[:, 1], qk_gain[1])
    packed = (
        jnp.stack([query, keyed, proj[:, 2]], axis=1)
        .astype(jnp.bfloat16)
        .reshape(rows, 3, heads * width)
    )
    cond_rows = cond_kv.shape[0]
    cond = cond_kv.reshape(cond_rows, 2, heads, width)
    cond_key = rms_gain(cond[:, 0].astype(jnp.float32), qk_gain[1]).astype(jnp.bfloat16)
    cond_pack = jnp.stack([cond_key, cond[:, 1]], axis=1).reshape(cond_rows, 2, heads * width)
    sent, cond_sent = (
        lax.all_to_all(packed, "sub", split_axis=2, concat_axis=0, tiled=True),
        lax.all_to_all(cond_pack, "sub", split_axis=2, concat_axis=0, tiled=True),
    )
    operands, start_state, absorb = arrange(sent, cond_sent, width)
    carry = absorb(
        start_state,
        (
            lax.all_gather(operands[0], "seq", axis=0, tiled=True),
            lax.all_gather(operands[1], "seq", axis=0, tiled=True),
            lax.all_gather(operands[2], "seq", axis=0, tiled=True),
            lax.all_gather(operands[3], "seq", axis=0, tiled=True),
        ),
        jnp.int32(0),
    )
    attended = lax.all_to_all(finish(carry), "sub", split_axis=0, concat_axis=1, tiled=True)
    return jnp.dot(attended, out_weight, preferred_element_type=jnp.float32).astype(jnp.bfloat16)


LANES = 128


def pair_norm(field, gain, half):
    low = lax.broadcasted_iota(jnp.int32, field.shape, 1) < half
    squares = field * field
    first = jnp.sum(jnp.where(low, squares, 0.0), axis=-1, keepdims=True)
    second = jnp.sum(jnp.where(low, 0.0, squares), axis=-1, keepdims=True)
    mean = jnp.where(low, first, second) * (1.0 / half)
    return field * lax.rsqrt(mean + 1e-06) * gain


def joint_kernel(
    seq, sub, half,
    latent, cond_kv, weight_hbm, gain, out_weight_hbm, out,
    weight, out_weight, send_kv, send_q, recv_kv, recv_q, value_t, answer, parts, attended,
    weight_sem, out_weight_sem, kv_sent, kv_here, q_sent, q_here, answer_sent, part_here,
):
    across = sub // 2
    pairs = seq * across
    count = 2 * pairs
    width = count * half
    rows, cond_rows = latent.shape[0], cond_kv.shape[0]
    held = rows + cond_rows
    my_seq, my_sub = lax.axis_index("seq"), lax.axis_index("sub")
    my_side, my_up = my_sub // across, lax.rem(my_sub, across)
    mine = my_seq * across + my_up
    me = my_side * pairs + mine
    other = (1 - my_side) * pairs

    def device(slot):
        pair = lax.rem(slot, pairs)
        side = slot // pairs
        return {"seq": pair // across, "sub": side * across + lax.rem(pair, across)}

    def pair_to(step):
        up = lax.rem(my_up + 1 + step // seq, across)
        return lax.rem(my_seq + 1 + lax.rem(step, seq), seq) * across + up

    def pair_from(step):
        up = lax.rem(my_up + 2 * across - 1 - step // seq, across)
        return lax.rem(my_seq + seq - 1 - lax.rem(step, seq), seq) * across + up

    def load(step, part):
        column = pl.multiple_of(part * width + pair_to(step) * LANES, LANES)
        return pltpu.make_async_copy(
            weight_hbm.at[:, pl.ds(column, LANES)],
            weight.at[step, :, pl.ds(part * LANES, LANES)],
            weight_sem.at[step, part],
        )

    def start_load(step, unused):
        for part in range(3):
            load(step, part).start()
        return unused

    lax.fori_loop(0, 2, start_load, 0)
    out_load = pltpu.make_async_copy(out_weight_hbm, out_weight, out_weight_sem)

    barrier = pltpu.get_barrier_semaphore()

    def greet(slot, unused):
        @pl.when(slot != me)
        def _():
            pl.semaphore_signal(barrier, inc=1, device_id=device(slot))

        return unused

    lax.fori_loop(0, count, greet, 0)

    def kv_copy(pair, landing):
        return pltpu.make_async_remote_copy(
            src_ref=send_kv.at[pair], dst_ref=recv_kv.at[landing],
            send_sem=kv_sent.at[pair], recv_sem=kv_here.at[landing],
            device_id=device(my_side * pairs + pair),
        )

    def q_copy(slot, landing):
        return pltpu.make_async_remote_copy(
            src_ref=send_q.at[lax.rem(slot, pairs)], dst_ref=recv_q.at[landing],
            send_sem=q_sent.at[slot], recv_sem=q_here.at[landing],
            device_id=device(slot),
        )

    def answer_copy(slot, landing):
        return pltpu.make_async_remote_copy(
            src_ref=answer.at[slot], dst_ref=parts.at[landing],
            send_sem=answer_sent.at[slot], recv_sem=part_here.at[landing],
            device_id=device(slot),
        )

    scale = float(half) ** -0.5

    def project(step, unused):
        pair = pair_to(step)
        column = pl.multiple_of(pair * LANES, LANES)
        for part in range(3):
            load(step, part).wait()

        @pl.when(step + 2 < pairs)
        def _():
            for part in range(3):
                load(step + 2, part).start()

        @pl.when(step == pairs - 1)
        def _():
            out_load.start()

        proj = jnp.dot(latent[...], weight[step], preferred_element_type=jnp.float32)
        query_gain = jnp.concatenate([gain[0, pl.ds(2 * pair + i, 1)] for i in range(2)], axis=1)
        key_gain = jnp.concatenate([gain[1, pl.ds(2 * pair + i, 1)] for i in range(2)], axis=1)
        query = pair_norm(proj[:, :LANES], query_gain, half) * scale
        send_q[pair] = query.astype(jnp.bfloat16).T
        keyed = pair_norm(proj[:, LANES : 2 * LANES], key_gain, half)
        send_kv[pair, :rows] = keyed.astype(jnp.bfloat16)
        cond_field = cond_kv[:, :, pl.ds(column, LANES)].astype(jnp.float32)
        cond_keyed = pair_norm(cond_field[:, 0], key_gain, half)
        send_kv[pair, rows:held] = cond_keyed.astype(jnp.bfloat16)
        send_kv[pair, held : held + rows] = proj[:, 2 * LANES :].astype(jnp.bfloat16)
        send_kv[pair, held + rows :] = cond_field[:, 1].astype(jnp.bfloat16)

        @pl.when(step == 0)
        def _():
            pl.semaphore_wait(barrier, count - 1)

        @pl.when(pair != mine)
        def _():
            kv_copy(pair, mine).start()

        q_copy(other + pair, me).start()

        @pl.when(pair == mine)
        def _():
            recv_kv[mine] = send_kv[mine]
            recv_q[me] = send_q[mine]

        return unused

    lax.fori_loop(0, pairs, project, 0)

    def send_near(step, unused):
        q_copy(my_side * pairs + pair_to(step), me).start()
        return unused

    lax.fori_loop(0, pairs - 1, send_near, 0)

    def receive(pair, unused):
        @pl.when(pair != mine)
        def _():
            kv_copy(pair, pair).wait_recv()

        return unused

    lax.fori_loop(0, pairs, receive, 0)

    value_t[...] = recv_kv[:, held:, :].reshape(pairs * held, LANES).T

    def attend(slots):
        keyed = recv_kv[:, :held, :].reshape(pairs * held, LANES)
        values = value_t[...]
        scores = []
        for slot in slots:
            query = recv_q[slot]
            low = lax.broadcasted_iota(jnp.int32, query.shape, 0) < half
            empty = jnp.zeros_like(query)
            query = jnp.concatenate(
                [jnp.where(low, query, empty), jnp.where(low, empty, query)], axis=1
            )
            scores.append(jnp.dot(keyed, query, preferred_element_type=jnp.float32))
        results = []
        for score in scores:
            highest = jnp.max(score, axis=0, keepdims=True)
            expd = jnp.exp(score - highest)
            total = jnp.sum(expd, axis=0, keepdims=True)
            summed = jnp.dot(
                values, expd.astype(jnp.bfloat16), preferred_element_type=jnp.float32
            )
            results.append((summed, highest, total))
        for slot, (summed, highest, total) in zip(slots, results):
            result = summed / total
            answer[slot, :half] = result[:half, :rows].astype(jnp.bfloat16)
            answer[slot, half : 2 * half] = result[half:, rows:].astype(jnp.bfloat16)
            left = highest + jnp.log(total)
            terms = []
            for unused in range(3):
                term = left.astype(jnp.bfloat16).astype(jnp.float32)
                left = left - term
                terms += [term[:, :rows], term[:, rows:]]
            terms.append(jnp.zeros((8 - len(terms), rows), jnp.float32))
            answer[slot, 2 * half :] = jnp.concatenate(terms, axis=0).astype(jnp.bfloat16)

    def attend_far(step, unused):
        slots = [other + pair_from(2 * step + i) for i in range(2)]
        for slot in slots:
            q_copy(slot, slot).wait_recv()
        attend(slots)
        for slot in slots:
            answer_copy(slot, me).start()
        return unused

    lax.fori_loop(0, pairs // 2, attend_far, 0)

    def attend_near(step, unused):
        slots = [my_side * pairs + pair_from(2 * step + i) for i in range(2)]
        for slot in slots:

            @pl.when(slot != me)
            def _():
                q_copy(slot, slot).wait_recv()

        attend(slots)
        for slot in slots:

            @pl.when(slot != me)
            def _():
                answer_copy(slot, me).start()

            @pl.when(slot == me)
            def _():
                parts[me] = answer[me]

        return unused

    lax.fori_loop(0, pairs // 2, attend_near, 0)
    out_load.wait()

    def logs(slot):
        stats = parts[slot, 2 * half :].astype(jnp.float32)
        return stats[0:2] + stats[2:4] + stats[4:6]

    def merge(step, unused):
        pair = pair_to(step)
        near, far = my_side * pairs + pair, other + pair
        answer_copy(far, far).wait_recv()

        @pl.when(near != me)
        def _():
            answer_copy(near, near).wait_recv()

        first, second = logs(near), logs(far)
        highest = jnp.maximum(first, second)
        first, second = jnp.exp(first - highest), jnp.exp(second - highest)
        both = first + second
        first, second = first / both, second / both
        merged = []
        for head in range(2):
            span = slice(head * half, (head + 1) * half)
            merged.append(
                parts[near, span].astype(jnp.float32) * first[head : head + 1]
                + parts[far, span].astype(jnp.float32) * second[head : head + 1]
            )
        merged = jnp.concatenate(merged, axis=0).astype(jnp.bfloat16)
        column = pl.multiple_of(pair * LANES, LANES)
        attended[:, pl.ds(column, LANES)] = merged.T
        return unused

    lax.fori_loop(0, pairs, merge, 0)

    out[...] = jnp.dot(
        attended[...], out_weight[...], preferred_element_type=jnp.float32
    ).astype(jnp.bfloat16)

    def drain(slot, unused):
        q_pair = lax.rem(slot, pairs)

        @pl.when(slot != me)
        def _():
            q_copy(slot, slot).wait_send()
            answer_copy(slot, slot).wait_send()

        @pl.when(jnp.logical_and(slot < pairs, q_pair != mine))
        def _():
            kv_copy(q_pair, q_pair).wait_send()

        return unused

    lax.fori_loop(0, count, drain, 0)


def pair_each(seq, sub, latent, cond_kv, qkv_weight, qk_gain, out_weight):
    rows, depth = latent.shape
    heads, half = qk_gain.shape[1:]
    cond_rows = cond_kv.shape[0]
    count = seq * sub
    pairs = count // 2
    held = rows + cond_rows
    vmem = pl.BlockSpec(memory_space=pltpu.VMEM)
    anywhere = pl.BlockSpec(memory_space=pl.ANY)
    narrow = jnp.bfloat16
    return pl.pallas_call(
        functools.partial(joint_kernel, seq, sub, half),
        out_shape=jax.ShapeDtypeStruct((rows, out_weight.shape[1]), narrow),
        in_specs=[vmem, vmem, anywhere, vmem, anywhere],
        out_specs=vmem,
        scratch_shapes=[
            pltpu.VMEM((pairs, depth, 3 * LANES), narrow),
            pltpu.VMEM(out_weight.shape, narrow),
            pltpu.VMEM((pairs, 2 * held, LANES), narrow),
            pltpu.VMEM((pairs, LANES, rows), narrow),
            pltpu.VMEM((pairs, 2 * held, LANES), narrow),
            pltpu.VMEM((count, LANES, rows), narrow),
            pltpu.VMEM((LANES, pairs * held), narrow),
            pltpu.VMEM((count, LANES + 8, rows), narrow),
            pltpu.VMEM((count, LANES + 8, rows), narrow),
            pltpu.VMEM((rows, heads * half), narrow),
            pltpu.SemaphoreType.DMA((pairs, 3)),
            pltpu.SemaphoreType.DMA,
            pltpu.SemaphoreType.DMA((pairs,)),
            pltpu.SemaphoreType.DMA((pairs,)),
            pltpu.SemaphoreType.DMA((count,)),
            pltpu.SemaphoreType.DMA((count,)),
            pltpu.SemaphoreType.DMA((count,)),
            pltpu.SemaphoreType.DMA((count,)),
        ],
        compiler_params=pltpu.CompilerParams(
            collective_id=0, has_side_effects=True, vmem_limit_bytes=60 * 1024 * 1024
        ),
    )(
        latent, cond_kv, qkv_weight,
        qk_gain, out_weight,
    )


def layer(seq, sub, latent, cond_kv, qkv_weight, qk_gain, out_weight):
    heads, width = qk_gain.shape[1:]
    fits = heads == seq * sub and 2 * width == LANES and latent.shape[0] == LANES
    fits = fits and sub % 2 == 0 and seq % 2 == 0 and cond_kv.shape[0] % 16 == 0
    if fits:
        return pair_each(seq, sub, latent, cond_kv, qkv_weight, qk_gain, out_weight)
    return local(latent, cond_kv, qkv_weight, qk_gain, out_weight)


def solution(mesh):
    return jax.shard_map(
        functools.partial(layer, mesh.shape["seq"], mesh.shape["sub"]),
        mesh=mesh,
        in_specs=(
            P(("clip", "seq", "sub"), None),
            P(("clip", "seq", "sub"), None, None),
            P(),
            P(),
            P(),
        ),
        out_specs=P(("clip", "seq", "sub"), None),
        check_vma=False,
    )
```

profile of v0, /device:TPU:0, one launch (start us, length us, event | category | flops | bytes accessed | tf_op | source)
XLA Modules:
  0.0 38.5 jit_solution(11232964527100238360)
XLA Ops:
  0.0 36.7 %shard_map.55 = bf16[128,1536]{1,0:T(8,128)(2,1)} custom-call(bf16[128,1536]{1,0:T(8,128)(2,1)} %latent.1, bf16[32,2,1024]{2,1,0:T(2,128)(2,1)} %cond_kv.1, bf16[1536,3072]{1,0:T(8,128)(2,1)} %weight_hbm.1, f32[2,16,64]{2,1,0:T(8,128)} %gain.1, bf16[1024,1536]{1,0:T(8,128)(2,1)} %out_weight_hbm.1), custom_call_target="tpu_custom_call" | custom-call | tf_op jit(solution)/shard_map/pallas_call | solution.py:398
  36.7 1.8 %copy.7 = bf16[128,1536]{1,0:T(8,128)(2,1)} copy(bf16[128,1536]{1,0:T(8,128)(2,1)} %shard_map.55) | data formatting | bytes 786432
where the time goes:
time: 38.8 us; the launch traced here: 38.5 us
  Pallas kernels  36.7 us (95%)
  local copies, waits for them, and re-layouts  1.77 us (5%)
    pallas_call x1, Pallas kernels, pair_each(): pl.pallas_call(functools.partial(joint_kernel, seq, sub, half), out_shape...  36.7 us
    unnamed x1, local copies, waits for them, and re-layouts  1.77 us

commit v1 on v0

--- a/solution.py
+++ b/solution.py
@@ -120,9 +120,9 @@
 
 def joint_kernel(
     seq, sub, half,
-    latent, cond_kv, weight_hbm, gain, out_weight_hbm, out,
-    weight, out_weight, send_kv, send_q, recv_kv, recv_q, value_t, answer, parts, attended,
-    weight_sem, out_weight_sem, kv_sent, kv_here, q_sent, q_here, answer_sent, part_here,
+    latent_hbm, cond_hbm, weight_hbm, gain_hbm, out_weight_hbm, out,
+    latent, cond_kv, gain, weight, out_weight, send_kv, send_q, recv_kv, recv_q, value_t, answer, parts, attended,
+    input_sem, weight_sem, out_weight_sem, kv_sent, kv_here, q_sent, q_here, answer_sent, part_here,
 ):
     across = sub // 2
     pairs = seq * across
@@ -162,6 +162,14 @@
             load(step, part).start()
         return unused
 
+    inputs = [
+        pltpu.make_async_copy(source, target, input_sem.at[i])
+        for i, (source, target) in enumerate(
+            [(latent_hbm, latent), (cond_hbm, cond_kv), (gain_hbm, gain)]
+        )
+    ]
+    for copy in inputs:
+        copy.start()
     lax.fori_loop(0, 2, start_load, 0)
     out_load = pltpu.make_async_copy(out_weight_hbm, out_weight, out_weight_sem)
 
@@ -198,6 +206,8 @@
         )
 
     scale = float(half) ** -0.5
+    for copy in inputs:
+        copy.wait()
 
     def project(step, unused):
         pair = pair_to(step)
@@ -393,14 +403,17 @@
     pairs = count // 2
     held = rows + cond_rows
     vmem = pl.BlockSpec(memory_space=pltpu.VMEM)
-    anywhere = pl.BlockSpec(memory_space=pl.ANY)
+    hbm = pl.BlockSpec(memory_space=pltpu.HBM)
     narrow = jnp.bfloat16
     return pl.pallas_call(
         functools.partial(joint_kernel, seq, sub, half),
         out_shape=jax.ShapeDtypeStruct((rows, out_weight.shape[1]), narrow),
-        in_specs=[vmem, vmem, anywhere, vmem, anywhere],
+        in_specs=[hbm] * 5,
         out_specs=vmem,
         scratch_shapes=[
+            pltpu.VMEM(latent.shape, narrow),
+            pltpu.VMEM(cond_kv.shape, narrow),
+            pltpu.VMEM(qk_gain.shape, jnp.float32),
             pltpu.VMEM((pairs, depth, 3 * LANES), narrow),
             pltpu.VMEM(out_weight.shape, narrow),
             pltpu.VMEM((pairs, 2 * held, LANES), narrow),
@@ -411,6 +424,7 @@
             pltpu.VMEM((count, LANES + 8, rows), narrow),
             pltpu.VMEM((count, LANES + 8, rows), narrow),
             pltpu.VMEM((rows, heads * half), narrow),
+            pltpu.SemaphoreType.DMA((3,)),
             pltpu.SemaphoreType.DMA((pairs, 3)),
             pltpu.SemaphoreType.DMA,
             pltpu.SemaphoreType.DMA((pairs,)),
@@ -421,11 +435,13 @@
             pltpu.SemaphoreType.DMA((count,)),
         ],
         compiler_params=pltpu.CompilerParams(
-            collective_id=0, has_side_effects=True, vmem_limit_bytes=60 * 1024 * 1024
+            collective_id=0, has_side_effects=True, vmem_limit_bytes=44 * 1024 * 1024
         ),
     )(
-        latent, cond_kv, qkv_weight,
-        qk_gain, out_weight,
+        *(
+            pltpu.with_memory_space_constraint(array, pltpu.HBM)
+            for array in (latent, cond_kv, qkv_weight, qk_gain, out_weight)
+        )
     )
 
 

time: 38.8 us -> 36.2 us (0.933)
  Pallas kernels: 36.7 us -> 35.2 us
  local copies, waits for them, and re-layouts: 1.77 us -> 0.75 us
    pallas_call x1, Pallas kernels: 36.7 us -> 35.2 us  [pair_each(): pl.pallas_call(functools.partial(joint_kernel, seq, sub, half), out_shape...]
    unnamed x1, local copies, waits for them, and re-layouts: 1.77 us -> 0.75 us
where the time goes in v1:
time: 36.2 us; the launch traced here: 35.9 us
  Pallas kernels  35.2 us (97%)
  local copies, waits for them, and re-layouts  0.75 us (2%)
    pallas_call x1, Pallas kernels, pair_each(): pl.pallas_call(functools.partial(joint_kernel, seq, sub, half), out_shape...  35.2 us
    unnamed x1, local copies, waits for them, and re-layouts  0.75 us

profile of v1, /device:TPU:0, one launch (start us, length us, event | category | flops | bytes accessed | tf_op | source)
XLA Modules:
  0.0 35.9 jit_solution(4579629434648026339)
XLA Ops:
  0.0 35.2 %shard_map.55 = bf16[128,1536]{1,0:T(8,128)(2,1)S(1)} custom-call(bf16[128,1536]{1,0:T(8,128)(2,1)} %latent_hbm.1, bf16[32,2,1024]{2,1,0:T(2,128)(2,1)} %cond_hbm.1, bf16[1536,3072]{1,0:T(8,128)(2,1)} %weight_hbm.1, f32[2,16,64]{2,1,0:T(8,128)} %gain_hbm.1, bf16[1024,1536]{1,0:T(8,128)(2,1)} %out_weight_hbm.1), custom_call_target="tpu_custom_call" | custom-call | tf_op jit(solution)/shard_map/pallas_call | solution.py:408
  35.2 0.7 %copy.7 = bf16[128,1536]{1,0:T(8,128)(2,1)} copy(bf16[128,1536]{1,0:T(8,128)(2,1)S(1)} %shard_map.55) | data formatting | bytes 786432

commit v2 on v1

--- a/solution.py
+++ b/solution.py
@@ -121,8 +121,8 @@
 def joint_kernel(
     seq, sub, half,
     latent_hbm, cond_hbm, weight_hbm, gain_hbm, out_weight_hbm, out,
-    latent, cond_kv, gain, weight, out_weight, send_kv, send_q, recv_kv, recv_q, value_t, answer, parts, attended,
-    input_sem, weight_sem, out_weight_sem, kv_sent, kv_here, q_sent, q_here, answer_sent, part_here,
+    latent, cond_kv, gain, weight, out_weight, send_kv_ref, send_q, recv_kv, recv_q, value_t, answer, parts, relayed, attended,
+    input_sem, weight_sem, out_weight_sem, kv_sent, kv_here, q_sent, q_here, answer_sent, part_here, relay_here, ready,
 ):
     across = sub // 2
     pairs = seq * across
@@ -145,10 +145,6 @@
         up = lax.rem(my_up + 1 + step // seq, across)
         return lax.rem(my_seq + 1 + lax.rem(step, seq), seq) * across + up
 
-    def pair_from(step):
-        up = lax.rem(my_up + 2 * across - 1 - step // seq, across)
-        return lax.rem(my_seq + seq - 1 - lax.rem(step, seq), seq) * across + up
-
     def load(step, part):
         column = pl.multiple_of(part * width + pair_to(step) * LANES, LANES)
         return pltpu.make_async_copy(
@@ -176,17 +172,23 @@
     barrier = pltpu.get_barrier_semaphore()
 
     def greet(slot, unused):
-        @pl.when(slot != me)
+        later = jnp.logical_or(my_side == 0, slot // pairs == 1)
+
+        @pl.when(jnp.logical_and(slot != me, later))
         def _():
             pl.semaphore_signal(barrier, inc=1, device_id=device(slot))
 
+        return unused
+
+    def announce(slot, unused):
+        pl.semaphore_signal(ready, inc=1, device_id=device(slot))
         return unused
 
     lax.fori_loop(0, count, greet, 0)
 
     def kv_copy(pair, landing):
         return pltpu.make_async_remote_copy(
-            src_ref=send_kv.at[pair], dst_ref=recv_kv.at[landing],
+            src_ref=send_kv_ref.at[pair], dst_ref=recv_kv.at[landing],
             send_sem=kv_sent.at[pair], recv_sem=kv_here.at[landing],
             device_id=device(my_side * pairs + pair),
         )
@@ -203,6 +205,16 @@
             src_ref=answer.at[slot], dst_ref=parts.at[landing],
             send_sem=answer_sent.at[slot], recv_sem=part_here.at[landing],
             device_id=device(slot),
+        )
+
+    outer = my_up == my_side
+
+    def relay_copy(slot):
+        seat = lax.rem(slot, pairs) // across
+        return pltpu.make_async_remote_copy(
+            src_ref=answer.at[slot], dst_ref=relayed.at[seat],
+            send_sem=answer_sent.at[slot], recv_sem=relay_here.at[seat],
+            device_id={"seq": my_seq, "sub": (1 - my_side) * across + my_side},
         )
 
     scale = float(half) ** -0.5
@@ -230,30 +242,66 @@
         query = pair_norm(proj[:, :LANES], query_gain, half) * scale
         send_q[pair] = query.astype(jnp.bfloat16).T
         keyed = pair_norm(proj[:, LANES : 2 * LANES], key_gain, half)
-        send_kv[pair, :rows] = keyed.astype(jnp.bfloat16)
+        send_kv_ref[pair, :rows] = keyed.astype(jnp.bfloat16)
         cond_field = cond_kv[:, :, pl.ds(column, LANES)].astype(jnp.float32)
         cond_keyed = pair_norm(cond_field[:, 0], key_gain, half)
-        send_kv[pair, rows:held] = cond_keyed.astype(jnp.bfloat16)
-        send_kv[pair, held : held + rows] = proj[:, 2 * LANES :].astype(jnp.bfloat16)
-        send_kv[pair, held + rows :] = cond_field[:, 1].astype(jnp.bfloat16)
-
-        @pl.when(step == 0)
-        def _():
-            pl.semaphore_wait(barrier, count - 1)
+        send_kv_ref[pair, rows:held] = cond_keyed.astype(jnp.bfloat16)
+        send_kv_ref[pair, held : held + rows] = proj[:, 2 * LANES :].astype(jnp.bfloat16)
+        send_kv_ref[pair, held + rows :] = cond_field[:, 1].astype(jnp.bfloat16)
+
+        @pl.when(step == start)
+        def _():
+            @pl.when(my_side == 0)
+            def _():
+                pl.semaphore_wait(barrier, pairs - 1)
+
+            @pl.when(my_side == 1)
+            def _():
+                pl.semaphore_wait(barrier, count - 1)
+                lax.fori_loop(0, pairs, announce, 0)
+
+            lax.fori_loop(0, step, send_kv, 0)
+
+        @pl.when(step >= start)
+        def _():
+            send_kv(step, 0)
+
+        @pl.when(step == opening)
+        def _():
+            @pl.when(my_side == 0)
+            def _():
+                pl.semaphore_wait(ready, pairs)
+
+            lax.fori_loop(0, step, send_far, 0)
+
+        @pl.when(step >= opening)
+        def _():
+            send_far(step, 0)
+
+        return unused
+
+    def send_kv(step, unused):
+        pair = pair_to(step)
 
         @pl.when(pair != mine)
         def _():
             kv_copy(pair, mine).start()
 
-        q_copy(other + pair, me).start()
-
         @pl.when(pair == mine)
         def _():
-            recv_kv[mine] = send_kv[mine]
+            recv_kv[mine] = send_kv_ref[mine]
             recv_q[me] = send_q[mine]
 
         return unused
 
+    def send_far(step, unused):
+        q_copy(other + pair_to(step), me).start()
+        return unused
+
+    start = jnp.where(my_sub == 0, 2, jnp.where(my_sub == 1, 0, 0))
+    late_opening = jnp.where(my_sub == across, 0, 7)
+    early_opening = jnp.where(my_sub == 0, 6, 5)
+    opening = jnp.where(my_side == 0, early_opening, late_opening)
     lax.fori_loop(0, pairs, project, 0)
 
     def send_near(step, unused):
@@ -307,55 +355,28 @@
             terms.append(jnp.zeros((8 - len(terms), rows), jnp.float32))
             answer[slot, 2 * half :] = jnp.concatenate(terms, axis=0).astype(jnp.bfloat16)
 
-    def attend_far(step, unused):
-        slots = [other + pair_from(2 * step + i) for i in range(2)]
-        for slot in slots:
-            q_copy(slot, slot).wait_recv()
-        attend(slots)
-        for slot in slots:
-            answer_copy(slot, me).start()
-        return unused
-
-    lax.fori_loop(0, pairs // 2, attend_far, 0)
-
-    def attend_near(step, unused):
-        slots = [my_side * pairs + pair_from(2 * step + i) for i in range(2)]
-        for slot in slots:
-
-            @pl.when(slot != me)
-            def _():
-                q_copy(slot, slot).wait_recv()
-
-        attend(slots)
-        for slot in slots:
-
-            @pl.when(slot != me)
-            def _():
-                answer_copy(slot, me).start()
-
-            @pl.when(slot == me)
-            def _():
-                parts[me] = answer[me]
-
-        return unused
-
-    lax.fori_loop(0, pairs // 2, attend_near, 0)
-    out_load.wait()
-
-    def logs(slot):
-        stats = parts[slot, 2 * half :].astype(jnp.float32)
+    def pick(table, quarter):
+        chosen = 0
+        for place in range(sub):
+            for i in range(4):
+                here = jnp.logical_and(my_sub == place, quarter == i)
+                chosen = jnp.where(here, table[place][i], chosen)
+        return chosen
+
+    def slot_at(turn, i):
+        place = 2 * turn + i
+        quarter = place // seq
+        far = pick([(1, 1, 0, 0), (1, 1, 0, 0), (1, 1, 0, 0), (1, 0, 1, 0)], quarter)
+        up = lax.rem(my_up + pick([(1, 0, 0, 1), (1, 0, 1, 0), (1, 0, 1, 0), (1, 1, 0, 0)], quarter), across)
+        seat = lax.rem(my_seq + 2 * seq - 1 - lax.rem(place, seq), seq)
+        return lax.rem(my_side + far, 2) * pairs + seat * across + up
+
+    def logs(stats):
+        stats = stats.astype(jnp.float32)
         return stats[0:2] + stats[2:4] + stats[4:6]
 
-    def merge(step, unused):
-        pair = pair_to(step)
-        near, far = my_side * pairs + pair, other + pair
-        answer_copy(far, far).wait_recv()
-
-        @pl.when(near != me)
-        def _():
-            answer_copy(near, near).wait_recv()
-
-        first, second = logs(near), logs(far)
+    def combine(near, far):
+        first, second = logs(near[2 * half :]), logs(far[2 * half :])
         highest = jnp.maximum(first, second)
         first, second = jnp.exp(first - highest), jnp.exp(second - highest)
         both = first + second
@@ -364,12 +385,69 @@
         for head in range(2):
             span = slice(head * half, (head + 1) * half)
             merged.append(
-                parts[near, span].astype(jnp.float32) * first[head : head + 1]
-                + parts[far, span].astype(jnp.float32) * second[head : head + 1]
+                near[span].astype(jnp.float32) * first[head : head + 1]
+                + far[span].astype(jnp.float32) * second[head : head + 1]
             )
-        merged = jnp.concatenate(merged, axis=0).astype(jnp.bfloat16)
+        return jnp.concatenate(merged, axis=0).astype(jnp.bfloat16)
+
+    def take(turn, unused):
+        slots = [slot_at(turn, i) for i in range(2)]
+        for slot in slots:
+
+            @pl.when(slot != me)
+            def _():
+                q_copy(slot, slot).wait_recv()
+
+        attend(slots)
+        for slot in slots:
+            side, up = slot // pairs, lax.rem(slot, across)
+            passing = jnp.logical_and(outer, side != my_side)
+            passing = jnp.logical_and(passing, up != my_side)
+            joining = jnp.logical_and(my_up != my_side, side == my_side)
+            joining = jnp.logical_and(joining, up == my_side)
+
+            @pl.when(joining)
+            def _():
+                relay_copy(slot).wait_recv()
+                seat = lax.rem(slot, pairs) // across
+                answer[slot, : 2 * half] = combine(answer[slot], relayed[seat])
+
+            @pl.when(passing)
+            def _():
+                relay_copy(slot).start()
+
+            @pl.when(jnp.logical_and(slot != me, jnp.logical_not(passing)))
+            def _():
+                answer_copy(slot, me).start()
+
+            @pl.when(slot == me)
+            def _():
+                parts[me] = answer[me]
+
+        return unused
+
+    lax.fori_loop(0, pairs, take, 0)
+    out_load.wait()
+
+    def merge(step, unused):
+        pair = pair_to(step)
+        near, far = my_side * pairs + pair, other + pair
         column = pl.multiple_of(pair * LANES, LANES)
-        attended[:, pl.ds(column, LANES)] = merged.T
+        whole = jnp.logical_and(outer, lax.rem(pair, across) != my_up)
+
+        @pl.when(near != me)
+        def _():
+            answer_copy(near, near).wait_recv()
+
+        @pl.when(whole)
+        def _():
+            attended[:, pl.ds(column, LANES)] = parts[near, : 2 * half].T
+
+        @pl.when(jnp.logical_not(whole))
+        def _():
+            answer_copy(far, far).wait_recv()
+            attended[:, pl.ds(column, LANES)] = combine(parts[near], parts[far]).T
+
         return unused
 
     lax.fori_loop(0, pairs, merge, 0)
@@ -423,6 +501,7 @@
             pltpu.VMEM((LANES, pairs * held), narrow),
             pltpu.VMEM((count, LANES + 8, rows), narrow),
             pltpu.VMEM((count, LANES + 8, rows), narrow),
+            pltpu.VMEM((seq, LANES + 8, rows), narrow),
             pltpu.VMEM((rows, heads * half), narrow),
             pltpu.SemaphoreType.DMA((3,)),
             pltpu.SemaphoreType.DMA((pairs, 3)),
@@ -433,6 +512,8 @@
             pltpu.SemaphoreType.DMA((count,)),
             pltpu.SemaphoreType.DMA((count,)),
             pltpu.SemaphoreType.DMA((count,)),
+            pltpu.SemaphoreType.DMA((seq,)),
+            pltpu.SemaphoreType.REGULAR,
         ],
         compiler_params=pltpu.CompilerParams(
             collective_id=0, has_side_effects=True, vmem_limit_bytes=44 * 1024 * 1024
@@ -448,7 +529,7 @@
 def layer(seq, sub, latent, cond_kv, qkv_weight, qk_gain, out_weight):
     heads, width = qk_gain.shape[1:]
     fits = heads == seq * sub and 2 * width == LANES and latent.shape[0] == LANES
-    fits = fits and sub % 2 == 0 and seq % 2 == 0 and cond_kv.shape[0] % 16 == 0
+    fits = fits and sub == 4 and seq % 2 == 0 and cond_kv.shape[0] % 16 == 0
     if fits:
         return pair_each(seq, sub, latent, cond_kv, qkv_weight, qk_gain, out_weight)
     return local(latent, cond_kv, qkv_weight, qk_gain, out_weight)

time: 36.2 us -> 35.2 us (0.972)
  Pallas kernels: 35.2 us -> 34.2 us
    pallas_call x1, Pallas kernels: 35.2 us -> 34.2 us  [pair_each(): pl.pallas_call(functools.partial(joint_kernel, seq, sub, half), out_shape...]
where the time goes in v2:
time: 35.2 us; the launch traced here: 35 us
  Pallas kernels  34.2 us (97%)
  local copies, waits for them, and re-layouts  0.75 us (2%)
    pallas_call x1, Pallas kernels, pair_each(): pl.pallas_call(functools.partial(joint_kernel, seq, sub, half), out_shape...  34.2 us
    unnamed x1, local copies, waits for them, and re-layouts  0.75 us

profile of v2, /device:TPU:0, one launch (start us, length us, event | category | flops | bytes accessed | tf_op | source)
XLA Modules:
  0.0 35.0 jit_solution(1388738759958812674)
XLA Ops:
  0.0 34.2 %shard_map.55 = bf16[128,1536]{1,0:T(8,128)(2,1)S(1)} custom-call(bf16[128,1536]{1,0:T(8,128)(2,1)} %latent_hbm.1, bf16[32,2,1024]{2,1,0:T(2,128)(2,1)} %cond_hbm.1, bf16[1536,3072]{1,0:T(8,128)(2,1)} %weight_hbm.1, f32[2,16,64]{2,1,0:T(8,128)} %gain_hbm.1, bf16[1024,1536]{1,0:T(8,128)(2,1)} %out_weight_hbm.1), custom_call_target="tpu_custom_call" | custom-call | tf_op jit(solution)/shard_map/pallas_call | solution.py:486
  34.2 0.7 %copy.7 = bf16[128,1536]{1,0:T(8,128)(2,1)} copy(bf16[128,1536]{1,0:T(8,128)(2,1)S(1)} %shard_map.55) | data formatting | bytes 786432
